TPU v7x, 32 devices: a whole 2x2x4 slice. The times are simulated.
32 devices in a mesh: blk: 16 (over z, x, core), tm: 2 (over y).
Axes of the slice: x: 2, y: 2, z: 4, core: 2. Of those that a mesh axis runs over, the one named last changes fastest.
Arguments:
- returns: bfloat16 [8192, 512], P('blk', 'tm'), may hold values from -6 to 6
- plan: int32 [2, 16], replicated, may hold values from 0 to 15, as said below
- pair_mask: int32 [16, 16], replicated, may hold values 0 or 1
Outputs:
- lead_lag: bfloat16 [8192, 2, 7680], P(('blk', 'tm'))
Inputs may be any that keep to these rules, and one draw needn't show every extreme that they name: Each round r has a word m_r with plan[r, b] = b XOR m_r for every block b; m_r is never 0, and every bit of a block index is set in the word of some round.
All inputs are finite; a program needn't handle non-finite values.
Results may differ from a plain program's by a relative error of at most 0.001.
Values may be sent and summed in bfloat16 or wider, within the bound.
A program may use at most 64 MiB of HBM per device.

v0:
```python
import jax
import jax.numpy as jnp
from jax import lax
from jax.sharding import PartitionSpec as P

LAG = 7
ROUNDS = 2


def swapped(block, axis, stride):
    count = lax.axis_size(axis)
    route = []
    for low in range(count):
        high = low | 1 << stride
        if high != low and high < count:
            route += [(low, high), (high, low)]
    return lax.ppermute(block, axis, route)


def on_device(returns, plan, pair_mask):
    own_block = lax.axis_index("blk")
    bit_count = lax.axis_size("blk").bit_length() - 1
    slab_count = lax.axis_size("tm")
    minutes = returns.shape[1]
    minutes_all = minutes * slab_count
    factor = float(minutes_all) ** (-0.5)
    collected = []
    own_part = lax.all_to_all(returns, "tm", split_axis=0, concat_axis=1, tiled=True)
    row_count = own_part.shape[0]
    own_padded = jnp.pad(own_part, ((0, 0), (LAG, LAG)))
    own_shifted = jnp.stack(
        [
            lax.slice_in_dim(own_padded, 2 * LAG - offset, 2 * LAG - offset + minutes_all, axis=1)
            for offset in range(2 * LAG + 1)
        ],
        axis=0,
    )
    for round_id in range(ROUNDS):
        mask_word = plan[round_id, 0]
        partner = jnp.bitwise_xor(own_block, mask_word)
        pair_live = pair_mask[own_block, partner]
        current = returns
        for bit in range(bit_count):
            flag = jnp.bitwise_and(jnp.right_shift(mask_word, bit), 1)
            arrived = swapped(current, "blk", bit)
            current = jnp.where(flag == 1, arrived, current)
        gathered = lax.all_gather(current, "tm", axis=1, tiled=True)
        tiles = lax.dot_general(
            own_shifted, gathered, (((2,), (1,)), ((), ())), preferred_element_type=jnp.float32
        )
        gram = jnp.transpose(tiles, (1, 0, 2)).reshape(row_count, -1)
        collected.append(gram * (factor * pair_live.astype(jnp.float32)))
    return jnp.stack(collected, axis=1).astype(jnp.bfloat16)


def solution(mesh):
    in_specs = (P("blk", "tm"), P(), P())
    out_specs = P(("blk", "tm"), None, None)
    return jax.shard_map(
        on_device, mesh=mesh, in_specs=in_specs, out_specs=out_specs, check_vma=False
    )
```

profile of v0, /device:TPU:30, one launch (start us, length us, event | category | flops | bytes accessed | tf_op | source)
XLA Modules:
  0.0 119.5 jit_solution(2978405132348421668)
XLA Ops:
  0.0 4.1 %all-to-all-start = ((bf16[2,256,256]{2,1,0:T(8,128)(2,1)}), bf16[2,256,256]{2,1,0:T(8,128)(2,1)S(1)}, u32[]{:S(2)}, u32[]{:S(2)}) async-start(bf16[2,256,256]{2,1,0:T(8,128)(2,1)} %bitcast.68), calls=%async_computation | async-start | bytes 524288 | tf_op jit(solution)/shard_map/all_to_all | solution.py:28
  4.1 1.3 %fusion.5 = (s32[1,1]{1,0:T(1,128)}, s32[1,1]{1,0:T(1,128)}) fusion(s32[2,16]{1,0:T(2,128)} %param.4), kind=kLoop, calls=%fused_computation.31 | loop fusion | bytes 16 | tf_op jit(solution)/shard_map/slice | solution.py:39
  11.4 1.4 %fusion.4 = (s32[1,1]{1,0:T(1,128)}, s32[1,1]{1,0:T(1,128)}) fusion(s32[16,16]{1,0:T(8,128)} %param.5, s32[]{:T(128)S(6)} %select_n.68, s32[]{:T(128)S(6)} %select_n.69, s32[]{:T(128)S(6)} %select_n.78), kind=kLoop, calls=%fused_computation.30 | loop fusion | bytes 28 | tf_op jit(solution)/shard_map/dynamic_slice | solution.py:41
  14.0 0.3 copy.9
  14.3 0.2 stack.61
  14.6 0.1 bitcast_dynamic-update-slice_fusion.12
  14.8 0.1 bitcast_dynamic-update-slice_fusion.11
  14.9 0.1 bitcast_dynamic-update-slice_fusion.10
  15.1 0.1 bitcast_dynamic-update-slice_fusion.9
  15.2 0.1 bitcast_dynamic-update-slice_fusion.8
  15.4 0.1 bitcast_dynamic-update-slice_fusion.7
  15.5 0.1 bitcast_dynamic-update-slice_fusion.6
  15.7 0.1 bitcast_dynamic-update-slice_fusion.5
  15.9 0.6 collective-permute-start.1
  16.9 1.6 %collective-permute-start.4 = (bf16[512,256]{1,0:T(8,128)(2,1)S(1)}, bf16[512,256]{1,0:T(8,128)(2,1)S(1)}, u32[]{:S(2)}, u32[]{:S(2)}) collective-permute-start(bf16[512,256]{1,0:T(8,128)(2,1)S(1)} %get-tuple-element.6), channel_id=1, source_target_pairs={{0,4},{4,0},{2,6},{6,2},{8,12},{12,8},{10,14},{14,10},{16,20},{20,... | collective-permute-start | bytes 786440 | tf_op jit(solution)/shard_map/ppermute | solution.py:17
  18.5 6.7 %collective-permute-done.1 = bf16[512,256]{1,0:T(8,128)(2,1)S(1)} collective-permute-done((bf16[512,256]{1,0:T(8,128)(2,1)S(1)}, bf16[512,256]{1,0:T(8,128)(2,1)S(1)}, u32[]{:S(2)}, u32[]{:S(2)}) %collective-permute-start.1) | collective-permute-done | bytes 262176 | tf_op jit(solution)/shard_map/ppermute | solution.py:17
  25.2 0.5 collective-permute-start.2
  25.8 4.5 %collective-permute-done.4 = bf16[512,256]{1,0:T(8,128)(2,1)S(1)} collective-permute-done((bf16[512,256]{1,0:T(8,128)(2,1)S(1)}, bf16[512,256]{1,0:T(8,128)(2,1)S(1)}, u32[]{:S(2)}, u32[]{:S(2)}) %collective-permute-start.4) | collective-permute-done | bytes 262176 | tf_op jit(solution)/shard_map/ppermute | solution.py:17
  30.3 0.5 collective-permute-start.5
  30.8 1.8 %collective-permute-done.2 = bf16[512,256]{1,0:T(8,128)(2,1)S(1)} collective-permute-done((bf16[512,256]{1,0:T(8,128)(2,1)S(1)}, bf16[512,256]{1,0:T(8,128)(2,1)S(1)}, u32[]{:S(2)}, u32[]{:S(2)}) %collective-permute-start.2) | collective-permute-done | bytes 262176 | tf_op jit(solution)/shard_map/ppermute | solution.py:17
  32.7 0.4 collective-permute-start.3
  33.2 8.5 %collective-permute-done.5 = bf16[512,256]{1,0:T(8,128)(2,1)S(1)} collective-permute-done((bf16[512,256]{1,0:T(8,128)(2,1)S(1)}, bf16[512,256]{1,0:T(8,128)(2,1)S(1)}, u32[]{:S(2)}, u32[]{:S(2)}) %collective-permute-start.5) | collective-permute-done | bytes 262176 | tf_op jit(solution)/shard_map/ppermute | solution.py:17
  41.8 0.3 collective-permute-start.6
  42.1 11.5 %collective-permute-done.3 = bf16[512,256]{1,0:T(8,128)(2,1)S(1)} collective-permute-done((bf16[512,256]{1,0:T(8,128)(2,1)S(1)}, bf16[512,256]{1,0:T(8,128)(2,1)S(1)}, u32[]{:S(2)}, u32[]{:S(2)}) %collective-permute-start.3) | collective-permute-done | bytes 262176 | tf_op jit(solution)/shard_map/ppermute | solution.py:17
  53.6 9.3 %all_gather.6 = bf16[512,512]{1,0:T(8,128)(2,1)S(1)} all-gather(bf16[512,256]{1,0:T(8,128)(2,1)S(1)} %broadcast_select_fusion.7), channel_id=1, replica_groups=mesh['blk'=16,'tm'=2] {'tm'}, dimensions={1}, use_global_device_ids=true | all-gather | bytes 786432 | tf_op jit(solution)/shard_map/all_gather | solution.py:47
  62.9 7.0 %all_gather.7 = bf16[512,512]{1,0:T(8,128)(2,1)S(1)} all-gather(bf16[512,256]{1,0:T(8,128)(2,1)S(1)} %broadcast_select_fusion.3), channel_id=1, replica_groups=mesh['blk'=16,'tm'=2] {'tm'}, dimensions={1}, use_global_device_ids=true | all-gather | bytes 786432 | tf_op jit(solution)/shard_map/all_gather | solution.py:47
  69.9 4.1 %fusion = bf16[256,15,512]{2,0,1:T(8,128)(2,1)} fusion(f32[]{:T(128)} %bitcast.18, bf16[15,256,512]{2,1,0:T(8,128)(2,1)S(1)} %bitcast_dynamic-update-slice_fusion, bf16[512,512]{1,0:T(8,128)(2,1)S(1)} %all_gather.6), kind=kOutput, calls=%fused_computation.3 | convolution fusion | flops 2017198080 | bytes 8388612 | tf_op jit(solution)/shard_map/dot_general | solution.py:48
  74.0 6.1 %copy.11 = bf16[256,15,512]{0,2,1:T(8,128)(2,1)} copy(bf16[256,15,512]{2,0,1:T(8,128)(2,1)} %fusion) | data formatting | bytes 7864320 | tf_op jit(solution)/shard_map/mul | solution.py:52
  80.1 6.2 %fusion.1 = bf16[256,15,512]{2,0,1:T(8,128)(2,1)} fusion(f32[]{:T(128)} %bitcast.23, bf16[15,256,512]{2,1,0:T(8,128)(2,1)} %copy-done.1, bf16[512,512]{1,0:T(8,128)(2,1)S(1)} %all_gather.7), kind=kOutput, calls=%fused_computation.4 | convolution fusion | flops 2017198080 | bytes 8388612 | tf_op jit(solution)/shard_map/dot_general | solution.py:48
  86.3 6.3 %copy.12 = bf16[256,15,512]{0,2,1:T(8,128)(2,1)} copy(bf16[256,15,512]{2,0,1:T(8,128)(2,1)} %fusion.1) | data formatting | bytes 7864320 | tf_op jit(solution)/shard_map/mul | solution.py:52
  92.6 7.1 %pad_maximum_fusion = bf16[256,2,7680]{0,2,1:T(8,128)(2,1)} fusion(bf16[256,1,7680]{0,2,1:T(8,128)(2,1)} %bitcast.65, bf16[256,1,7680]{0,2,1:T(8,128)(2,1)} %bitcast.64), kind=kLoop, calls=%fused_computation | loop fusion | flops 3932160 | bytes 15728640 | tf_op jit(solution)/shard_map/stack | solution.py:53
  99.7 19.8 %copy.13 = bf16[256,2,7680]{2,1,0:T(2,128)(2,1)} copy(bf16[256,2,7680]{0,2,1:T(8,128)(2,1)} %pad_maximum_fusion) | data formatting | bytes 15728640 | tf_op jit(solution)/shard_map/stack | solution.py:53
  (23 shorter events, 1.1 us)
Async XLA Ops:
  0.0 15.8 %copy-start = (bf16[512,256]{1,0:T(8,128)(2,1)S(1)}, bf16[512,256]{1,0:T(8,128)(2,1)}, u32[]{:S(2)}) copy-start(bf16[512,256]{1,0:T(8,128)(2,1)} %param.3) | copy-start | bytes 786436
  0.0 14.0 %all-to-all-start = ((bf16[2,256,256]{2,1,0:T(8,128)(2,1)}), bf16[2,256,256]{2,1,0:T(8,128)(2,1)S(1)}, u32[]{:S(2)}, u32[]{:S(2)}) async-start(bf16[2,256,256]{2,1,0:T(8,128)(2,1)} %bitcast.68), calls=%async_computation | async-start | bytes 524288 | tf_op jit(solution)/shard_map/all_to_all | solution.py:28
  4.1 11.7 %collective-permute-start = (bf16[512,256]{1,0:T(8,128)(2,1)}, bf16[512,256]{1,0:T(8,128)(2,1)S(1)}, u32[]{:S(2)}, u32[]{:S(2)}) collective-permute-start(bf16[512,256]{1,0:T(8,128)(2,1)} %param.3), channel_id=1, source_target_pairs={{0,2},{2,0},{4,6},{6,4},{8,10},{10,8},{12,14},{14,12},{16,18},{18,... | collective-permute-start | bytes 786440 | tf_op jit(solution)/shard_map/ppermute | solution.py:17
  15.9 9.2 %collective-permute-start.1 = (bf16[512,256]{1,0:T(8,128)(2,1)S(1)}, bf16[512,256]{1,0:T(8,128)(2,1)S(1)}, u32[]{:S(2)}, u32[]{:S(2)}) collective-permute-start(bf16[512,256]{1,0:T(8,128)(2,1)S(1)} %get-tuple-element.5), channel_id=1, source_target_pairs={{0,4},{4,0},{2,6},{6,2},{8,12},{12,8},{10,14},{14,10},{16,20},{20,... | collective-permute-start | bytes 786440 | tf_op jit(solution)/shard_map/ppermute | solution.py:17
  16.9 13.4 %collective-permute-start.4 = (bf16[512,256]{1,0:T(8,128)(2,1)S(1)}, bf16[512,256]{1,0:T(8,128)(2,1)S(1)}, u32[]{:S(2)}, u32[]{:S(2)}) collective-permute-start(bf16[512,256]{1,0:T(8,128)(2,1)S(1)} %get-tuple-element.6), channel_id=1, source_target_pairs={{0,4},{4,0},{2,6},{6,2},{8,12},{12,8},{10,14},{14,10},{16,20},{20,... | collective-permute-start | bytes 786440 | tf_op jit(solution)/shard_map/ppermute | solution.py:17
  25.2 7.5 %collective-permute-start.2 = (bf16[512,256]{1,0:T(8,128)(2,1)S(1)}, bf16[512,256]{1,0:T(8,128)(2,1)S(1)}, u32[]{:S(2)}, u32[]{:S(2)}) collective-permute-start(bf16[512,256]{1,0:T(8,128)(2,1)S(1)} %broadcast_select_fusion.5), channel_id=1, source_target_pairs={{0,8},{8,0},{2,10},{10,2},{4,12},{12,4},{6,14},{14,6},{16,24},{24,... | collective-permute-start | bytes 786440 | tf_op jit(solution)/shard_map/ppermute | solution.py:17
  30.3 11.4 %collective-permute-start.5 = (bf16[512,256]{1,0:T(8,128)(2,1)S(1)}, bf16[512,256]{1,0:T(8,128)(2,1)S(1)}, u32[]{:S(2)}, u32[]{:S(2)}) collective-permute-start(bf16[512,256]{1,0:T(8,128)(2,1)S(1)} %broadcast_select_fusion.1), channel_id=1, source_target_pairs={{0,8},{8,0},{2,10},{10,2},{4,12},{12,4},{6,14},{14,6},{16,24},{24,... | collective-permute-start | bytes 786440 | tf_op jit(solution)/shard_map/ppermute | solution.py:17
  32.7 20.9 %collective-permute-start.3 = (bf16[512,256]{1,0:T(8,128)(2,1)S(1)}, bf16[512,256]{1,0:T(8,128)(2,1)S(1)}, u32[]{:S(2)}, u32[]{:S(2)}) collective-permute-start(bf16[512,256]{1,0:T(8,128)(2,1)S(1)} %broadcast_select_fusion.6), channel_id=1, source_target_pairs={{0,16},{16,0},{2,18},{18,2},{4,20},{20,4},{6,22},{22,6},{8,24},{24... | collective-permute-start | bytes 786440 | tf_op jit(solution)/shard_map/ppermute | solution.py:17
  33.2 36.7 %copy-start.1 = (bf16[15,256,512]{2,1,0:T(8,128)(2,1)}, bf16[15,256,512]{2,1,0:T(8,128)(2,1)S(1)}, u32[]{:S(2)}) copy-start(bf16[15,256,512]{2,1,0:T(8,128)(2,1)S(1)} %bitcast_dynamic-update-slice_fusion) | copy-start | bytes 11796484
  41.8 21.1 %collective-permute-start.6 = (bf16[512,256]{1,0:T(8,128)(2,1)S(1)}, bf16[512,256]{1,0:T(8,128)(2,1)S(1)}, u32[]{:S(2)}, u32[]{:S(2)}) collective-permute-start(bf16[512,256]{1,0:T(8,128)(2,1)S(1)} %broadcast_select_fusion.2), channel_id=1, source_target_pairs={{0,16},{16,0},{2,18},{18,2},{4,20},{20,4},{6,22},{22,6},{8,24},{24... | collective-permute-start | bytes 786440 | tf_op jit(solution)/shard_map/ppermute | solution.py:17
where the time goes:
time: 121 us; the launch traced here: 120 us
  local copies, waits for them, and re-layouts  37.2 us (31%)
  waiting for transfers between devices  33 us (27%)
  blocking collectives  16.3 us (13%)
  matrix products  10.3 us (9%)
  starting transfers between devices  7.91 us (7%)
  between operations  7.48 us (6%)
  other arithmetic  7.3 us (6%)
    ppermute x7, waiting for transfers between devices, swapped(): return lax.ppermute(block, axis, route)  33 us
    another operation x1, local copies, waits for them, and re-layouts, on_device(): return jnp.stack(collected, axis=1).astype(jnp.bfloat16)  19.8 us
    all_gather x2, blocking collectives, on_device(): gathered = lax.all_gather(current, 'tm', axis=1, tiled=True)  16.3 us
    mul x2, local copies, waits for them, and re-layouts, on_device(): collected.append(gram * (factor * pair_live.astype(jnp.float32)))  12.3 us
    dot_general x2, matrix products, on_device(): lax.dot_general(own_shifted, gathered, (((2,), (1,)), ((), ())), preferre...  10.3 us
    another operation x1, other arithmetic, on_device(): return jnp.stack(collected, axis=1).astype(jnp.bfloat16)  7.08 us
    all_to_all x1, starting transfers between devices, on_device(): lax.all_to_all(returns, 'tm', split_axis=0, concat_axis=1, tiled=True)  4.07 us
    ppermute x7, starting transfers between devices, swapped(): return lax.ppermute(block, axis, route)  3.84 us
  transfers between devices with their start and end apart: 8, of which 5 were waited for; matrix products, arithmetic and copies ran while one was open for 4% of the time, Pallas kernels for 0%

commit v1 on v0

v1 whole, which is shorter than its diff:
```python
import functools

import jax
import jax.numpy as jnp
from jax import lax
from jax.experimental import pallas as pl
from jax.experimental.pallas import tpu as pltpu
from jax.experimental.layout import Layout, with_layout_constraint
from jax.sharding import PartitionSpec as P

LAG = 7
LAGS = 2 * LAG + 1
ROUNDS = 2
LANES = 128


def swapped(block, axis, stride):
    count = lax.axis_size(axis)
    route = []
    for low in range(count):
        high = low | 1 << stride
        if high != low and high < count:
            route += [(low, high), (high, low)]
    return lax.ppermute(block, axis, route)


def gram_kernel(bi, own_ref, first_ref, second_ref, scale_ref, out_ref, mates, lhs, packed):
    slabs, rows, minutes = own_ref.shape
    width = mates.shape[1]
    total = slabs * minutes
    step = pl.program_id(0)
    groups = width // LANES
    pitch = LAGS * groups * ROUNDS

    @pl.when(step == 0)
    def _():
        for s in range(slabs):
            mates[0, :, s * minutes:(s + 1) * minutes] = first_ref[s]
            mates[1, :, s * minutes:(s + 1) * minutes] = second_ref[s]

    start = pl.multiple_of(step * bi, bi)
    own = jnp.concatenate([own_ref[s, pl.ds(start, bi), :] for s in range(slabs)], axis=1)
    own = own.astype(jnp.float32)
    lane = lax.broadcasted_iota(jnp.int32, (bi, total), 1)
    for k in range(LAGS):
        lag = k - LAG
        if lag == 0:
            moved = own
        else:
            moved = pltpu.roll(own, lag % total, 1)
            keep = lane >= lag if lag > 0 else lane < total + lag
            moved = jnp.where(keep, moved, 0.0)
        lhs[k * bi:(k + 1) * bi, :] = moved.astype(lhs.dtype)
    for r in range(ROUNDS):
        gram = lax.dot_general(
            lhs[...], mates[r], (((1,), (1,)), ((), ())), preferred_element_type=jnp.float32
        ) * scale_ref[r]
        for k in range(LAGS):
            for c in range(groups):
                packed[pl.ds((k * groups + c) * ROUNDS + r, bi, stride=pitch), :] = gram[
                    k * bi:(k + 1) * bi, c * LANES:(c + 1) * LANES
                ]
    out_ref[...] = packed[...].astype(out_ref.dtype)


def gram_call(own, first, second, scale):
    slabs, rows, minutes = own.shape
    width = first.shape[1]
    total = slabs * minutes
    bi = min(32, rows)
    pitch = LAGS * (width // LANES) * ROUNDS
    whole = lambda a: pl.BlockSpec(a.shape, lambda i: (0, 0, 0))
    flat = pl.pallas_call(
        functools.partial(gram_kernel, bi),
        grid=(rows // bi,),
        in_specs=[
            whole(own), whole(first), whole(second),
            pl.BlockSpec(memory_space=pltpu.SMEM),
        ],
        out_specs=pl.BlockSpec((bi * pitch, LANES), lambda i: (i, 0)),
        out_shape=jax.ShapeDtypeStruct((rows * pitch, LANES), jnp.bfloat16),
        scratch_shapes=[
            pltpu.VMEM((ROUNDS, width, total), jnp.bfloat16),
            pltpu.VMEM((LAGS * bi, total), jnp.bfloat16),
            pltpu.VMEM((bi * pitch, LANES), jnp.float32),
        ],
        compiler_params=pltpu.CompilerParams(vmem_limit_bytes=48 * 2**20),
    )(own, first, second, scale)
    tiles = flat.reshape(rows, pitch // ROUNDS, ROUNDS, LANES)
    tiles = with_layout_constraint(tiles, Layout(major_to_minor=(0, 1, 2, 3)))
    return tiles.transpose(0, 2, 1, 3).reshape(rows, ROUNDS, LAGS * width)


def on_device(returns, plan, pair_mask):
    own_block = lax.axis_index("blk")
    bit_count = lax.axis_size("blk").bit_length() - 1
    slab_count = lax.axis_size("tm")
    width, minutes = returns.shape
    factor = float(minutes * slab_count) ** (-0.5)
    own = lax.all_to_all(
        returns.reshape(slab_count, width // slab_count, minutes), "tm", split_axis=0, concat_axis=0
    )
    mates, scales = [], []
    for round_id in range(ROUNDS):
        mask_word = plan[round_id, 0]
        partner = jnp.bitwise_xor(own_block, mask_word)
        scales.append(factor * pair_mask[own_block, partner].astype(jnp.float32))
        current = returns
        for bit in range(bit_count):
            flag = jnp.bitwise_and(jnp.right_shift(mask_word, bit), 1)
            arrived = swapped(current, "blk", bit)
            current = jnp.where(flag == 1, arrived, current)
        mates.append(lax.all_gather(current, "tm", axis=0))
    return gram_call(own, mates[0], mates[1], jnp.stack(scales))


def solution(mesh):
    in_specs = (P("blk", "tm"), P(), P())
    out_specs = P(("blk", "tm"), None, None)
    return jax.shard_map(
        on_device, mesh=mesh, in_specs=in_specs, out_specs=out_specs, check_vma=False
    )
```

time: 121 us -> 70.2 us (0.58)
  the two profiles are of different devices: /device:TPU:30 before, /device:TPU:28 now
where the time goes in v1:
time: 70.2 us; the launch traced here: 69.8 us
  waiting for transfers between devices  22.8 us (32%)
  blocking collectives  15.9 us (23%)
  starting transfers between devices  10.6 us (15%)
  Pallas kernels  8.92 us (13%)
  between operations  7.64 us (11%)
  local copies, waits for them, and re-layouts  2.71 us (4%)
  other arithmetic  1.24 us (2%)
    ppermute x7, waiting for transfers between devices, swapped(): return lax.ppermute(block, axis, route)  22.8 us
    all_gather x2, blocking collectives, on_device(): mates.append(lax.all_gather(current, 'tm', axis=0))  15.9 us
    pallas_call x1, Pallas kernels, gram_call(): pl.pallas_call(functools.partial(gram_kernel, bi), grid=(rows // bi,), in...  8.92 us
    ppermute x7, starting transfers between devices, swapped(): return lax.ppermute(block, axis, route)  6.65 us
    all_to_all x1, starting transfers between devices, on_device(): lax.all_to_all(returns.reshape(slab_count, width // slab_count, minutes),...  3.94 us
  transfers between devices with their start and end apart: 8, of which 3 were waited for; matrix products, arithmetic and copies ran while one was open for 4% of the time, Pallas kernels for 0%

profile of v1, /device:TPU:28, one launch (start us, length us, event | category | flops | bytes accessed | tf_op | source)
XLA Modules:
  0.0 69.8 jit_solution(4867778345893866121)
XLA Ops:
  0.0 0.0 collective-permute-start
  0.0 1.3 %fusion.1 = (s32[1,1]{1,0:T(1,128)}, s32[1,1]{1,0:T(1,128)}) fusion(s32[2,16]{1,0:T(2,128)} %param.4), kind=kLoop, calls=%fused_computation.10 | loop fusion | bytes 16 | tf_op jit(solution)/shard_map/slice | solution.py:105
  2.6 0.0 collective-permute-done
  2.6 1.0 %broadcast_select_fusion = (bf16[512,256]{1,0:T(8,128)(2,1)S(1)}, bf16[512,256]{1,0:T(8,128)(2,1)S(1)}) fusion(bf16[512,256]{1,0:T(8,128)(2,1)S(1)} %collective-permute-done, bf16[512,256]{1,0:T(8,128)(2,1)} %param.3, pred[]{:T(512)S(6)} %eq.31, pred[]{:T(512)S(6)} %eq.27), kind=kLoop, calls=%fused_computation | loop fusion | flops 262144 | bytes 1048578 | tf_op jit(solution)/shard_map/jit(_where)/select_n | solution.py:112
  3.6 1.6 %collective-permute-start.4 = (bf16[512,256]{1,0:T(8,128)(2,1)S(1)}, bf16[512,256]{1,0:T(8,128)(2,1)S(1)}, u32[]{:S(2)}, u32[]{:S(2)}) collective-permute-start(bf16[512,256]{1,0:T(8,128)(2,1)S(1)} %get-tuple-element.5), channel_id=1, source_target_pairs={{0,4},{4,0},{2,6},{6,2},{8,12},{12,8},{10,14},{14,10},{16,20},{20,... | collective-permute-start | bytes 786440 | tf_op jit(solution)/shard_map/ppermute | solution.py:24
  5.8 0.6 collective-permute-start.1
  6.4 6.4 %collective-permute-done.4 = bf16[512,256]{1,0:T(8,128)(2,1)S(1)} collective-permute-done((bf16[512,256]{1,0:T(8,128)(2,1)S(1)}, bf16[512,256]{1,0:T(8,128)(2,1)S(1)}, u32[]{:S(2)}, u32[]{:S(2)}) %collective-permute-start.4) | collective-permute-done | bytes 262176 | tf_op jit(solution)/shard_map/ppermute | solution.py:24
  12.9 0.5 collective-permute-start.5
  13.4 3.9 %all-to-all-start = ((bf16[2,256,256]{2,1,0:T(8,128)(2,1)}), bf16[2,256,256]{2,1,0:T(8,128)(2,1)S(1)}, u32[]{:S(2)}, u32[]{:S(2)}) async-start(bf16[2,256,256]{2,1,0:T(8,128)(2,1)} %bitcast.14), calls=%async_computation | async-start | bytes 524288 | tf_op jit(solution)/shard_map/all_to_all | solution.py:100
  19.9 1.4 %fusion = (s32[1,1]{1,0:T(1,128)}, s32[1,1]{1,0:T(1,128)}) fusion(s32[16,16]{1,0:T(8,128)} %param.5, s32[]{:T(128)S(6)} %select_n.76, s32[]{:T(128)S(6)} %select_n.77, s32[]{:T(128)S(6)} %select_n.78), kind=kLoop, calls=%fused_computation.9 | loop fusion | bytes 28 | tf_op jit(solution)/shard_map/dynamic_slice | solution.py:107
  22.5 0.0 collective-permute-done.1
  22.5 1.6 %collective-permute-start.2 = (bf16[512,256]{1,0:T(8,128)(2,1)S(1)}, bf16[512,256]{1,0:T(8,128)(2,1)S(1)}, u32[]{:S(2)}, u32[]{:S(2)}) collective-permute-start(bf16[512,256]{1,0:T(8,128)(2,1)S(1)} %broadcast_select_fusion.5), channel_id=1, source_target_pairs={{0,8},{8,0},{2,10},{10,2},{4,12},{12,4},{6,14},{14,6},{16,24},{24,... | collective-permute-start | bytes 786440 | tf_op jit(solution)/shard_map/ppermute | solution.py:24
  24.2 0.0 collective-permute-done.5
  24.2 0.4 collective-permute-start.6
  24.6 0.1 pad_maximum_fusion.scale_ref
  26.6 6.0 %collective-permute-done.2 = bf16[512,256]{1,0:T(8,128)(2,1)S(1)} collective-permute-done((bf16[512,256]{1,0:T(8,128)(2,1)S(1)}, bf16[512,256]{1,0:T(8,128)(2,1)S(1)}, u32[]{:S(2)}, u32[]{:S(2)}) %collective-permute-start.2) | collective-permute-done | bytes 262176 | tf_op jit(solution)/shard_map/ppermute | solution.py:24
  32.6 1.9 %collective-permute-start.3 = (bf16[512,256]{1,0:T(8,128)(2,1)S(1)}, bf16[512,256]{1,0:T(8,128)(2,1)S(1)}, u32[]{:S(2)}, u32[]{:S(2)}) collective-permute-start(bf16[512,256]{1,0:T(8,128)(2,1)S(1)} %broadcast_select_fusion.6), channel_id=1, source_target_pairs={{0,16},{16,0},{2,18},{18,2},{4,20},{20,4},{6,22},{22,6},{8,24},{24... | collective-permute-start | bytes 786440 | tf_op jit(solution)/shard_map/ppermute | solution.py:24
  34.6 10.3 %collective-permute-done.6 = bf16[512,256]{1,0:T(8,128)(2,1)S(1)} collective-permute-done((bf16[512,256]{1,0:T(8,128)(2,1)S(1)}, bf16[512,256]{1,0:T(8,128)(2,1)S(1)}, u32[]{:S(2)}, u32[]{:S(2)}) %collective-permute-start.6) | collective-permute-done | bytes 262176 | tf_op jit(solution)/shard_map/ppermute | solution.py:24
  44.9 8.9 %all-gather.1 = bf16[1024,256]{1,0:T(8,128)(2,1)S(1)} all-gather(bf16[512,256]{1,0:T(8,128)(2,1)S(1)} %broadcast_select_fusion.3), channel_id=3, replica_groups=mesh['blk'=16,'tm'=2] {'tm'}, dimensions={0}, use_global_device_ids=true | all-gather | bytes 786432 | tf_op jit(solution)/shard_map/all_gather | solution.py:113
  53.8 0.0 collective-permute-done.3
  53.8 7.0 %all-gather = bf16[1024,256]{1,0:T(8,128)(2,1)S(1)} all-gather(bf16[512,256]{1,0:T(8,128)(2,1)S(1)} %broadcast_select_fusion.7), channel_id=2, replica_groups=mesh['blk'=16,'tm'=2] {'tm'}, dimensions={0}, use_global_device_ids=true | all-gather | bytes 786432 | tf_op jit(solution)/shard_map/all_gather | solution.py:113
  60.9 0.0 all-to-all-done.own_ref
  60.9 8.9 %shard_map.37 = bf16[30720,128]{1,0:T(8,128)(2,1)} custom-call(bf16[2,256,256]{2,1,0:T(8,128)(2,1)S(1)} %all-to-all-done.own_ref, bf16[2,512,256]{2,1,0:T(8,128)(2,1)S(1)} %bitcast.13, bf16[2,512,256]{2,1,0:T(8,128)(2,1)S(1)} %bitcast.12, f32[2]{0:T(128)S(1)} %pad_maximum_fusion.scale_ref), custom_call_target="tpu_custom_call" | custom-call | tf_op jit(solution)/shard_map/pallas_call | solution.py:73
  (6 shorter events, 0.2 us)
Async XLA Ops:
  0.0 2.6 %collective-permute-start = (bf16[512,256]{1,0:T(8,128)(2,1)}, bf16[512,256]{1,0:T(8,128)(2,1)S(1)}, u32[]{:S(2)}, u32[]{:S(2)}) collective-permute-start(bf16[512,256]{1,0:T(8,128)(2,1)} %param.3), channel_id=1, source_target_pairs={{0,2},{2,0},{4,6},{6,4},{8,10},{10,8},{12,14},{14,12},{16,18},{18,... | collective-permute-start | bytes 786440 | tf_op jit(solution)/shard_map/ppermute | solution.py:24
  3.6 9.2 %collective-permute-start.4 = (bf16[512,256]{1,0:T(8,128)(2,1)S(1)}, bf16[512,256]{1,0:T(8,128)(2,1)S(1)}, u32[]{:S(2)}, u32[]{:S(2)}) collective-permute-start(bf16[512,256]{1,0:T(8,128)(2,1)S(1)} %get-tuple-element.5), channel_id=1, source_target_pairs={{0,4},{4,0},{2,6},{6,2},{8,12},{12,8},{10,14},{14,10},{16,20},{20,... | collective-permute-start | bytes 786440 | tf_op jit(solution)/shard_map/ppermute | solution.py:24
  5.8 16.7 %collective-permute-start.1 = (bf16[512,256]{1,0:T(8,128)(2,1)S(1)}, bf16[512,256]{1,0:T(8,128)(2,1)S(1)}, u32[]{:S(2)}, u32[]{:S(2)}) collective-permute-start(bf16[512,256]{1,0:T(8,128)(2,1)S(1)} %get-tuple-element.6), channel_id=1, source_target_pairs={{0,4},{4,0},{2,6},{6,2},{8,12},{12,8},{10,14},{14,10},{16,20},{20,... | collective-permute-start | bytes 786440 | tf_op jit(solution)/shard_map/ppermute | solution.py:24
  12.9 11.3 %collective-permute-start.5 = (bf16[512,256]{1,0:T(8,128)(2,1)S(1)}, bf16[512,256]{1,0:T(8,128)(2,1)S(1)}, u32[]{:S(2)}, u32[]{:S(2)}) collective-permute-start(bf16[512,256]{1,0:T(8,128)(2,1)S(1)} %broadcast_select_fusion.1), channel_id=1, source_target_pairs={{0,8},{8,0},{2,10},{10,2},{4,12},{12,4},{6,14},{14,6},{16,24},{24,... | collective-permute-start | bytes 786440 | tf_op jit(solution)/shard_map/ppermute | solution.py:24
  13.4 47.5 %all-to-all-start = ((bf16[2,256,256]{2,1,0:T(8,128)(2,1)}), bf16[2,256,256]{2,1,0:T(8,128)(2,1)S(1)}, u32[]{:S(2)}, u32[]{:S(2)}) async-start(bf16[2,256,256]{2,1,0:T(8,128)(2,1)} %bitcast.14), calls=%async_computation | async-start | bytes 524288 | tf_op jit(solution)/shard_map/all_to_all | solution.py:100
  22.5 10.1 %collective-permute-start.2 = (bf16[512,256]{1,0:T(8,128)(2,1)S(1)}, bf16[512,256]{1,0:T(8,128)(2,1)S(1)}, u32[]{:S(2)}, u32[]{:S(2)}) collective-permute-start(bf16[512,256]{1,0:T(8,128)(2,1)S(1)} %broadcast_select_fusion.5), channel_id=1, source_target_pairs={{0,8},{8,0},{2,10},{10,2},{4,12},{12,4},{6,14},{14,6},{16,24},{24,... | collective-permute-start | bytes 786440 | tf_op jit(solution)/shard_map/ppermute | solution.py:24
  24.2 20.7 %collective-permute-start.6 = (bf16[512,256]{1,0:T(8,128)(2,1)S(1)}, bf16[512,256]{1,0:T(8,128)(2,1)S(1)}, u32[]{:S(2)}, u32[]{:S(2)}) collective-permute-start(bf16[512,256]{1,0:T(8,128)(2,1)S(1)} %broadcast_select_fusion.2), channel_id=1, source_target_pairs={{0,16},{16,0},{2,18},{18,2},{4,20},{20,4},{6,22},{22,6},{8,24},{24... | collective-permute-start | bytes 786440 | tf_op jit(solution)/shard_map/ppermute | solution.py:24
  32.6 21.1 %collective-permute-start.3 = (bf16[512,256]{1,0:T(8,128)(2,1)S(1)}, bf16[512,256]{1,0:T(8,128)(2,1)S(1)}, u32[]{:S(2)}, u32[]{:S(2)}) collective-permute-start(bf16[512,256]{1,0:T(8,128)(2,1)S(1)} %broadcast_select_fusion.6), channel_id=1, source_target_pairs={{0,16},{16,0},{2,18},{18,2},{4,20},{20,4},{6,22},{22,6},{8,24},{24... | collective-permute-start | bytes 786440 | tf_op jit(solution)/shard_map/ppermute | solution.py:24
